TPU v7x, 256 devices: a whole 4x4x8 slice. The times are simulated.
256 devices in a mesh: row: 8 (over x_lo, y), col: 32 (over z, x_hi, core).
Axes of the slice: x: 4 (x_hi: 2, x_lo: 2; x = x_hi * 2 + x_lo), y: 4, z: 8, core: 2. Of those that a mesh axis runs over, the one named last changes fastest.
Arguments:
- b_steps: float32 [2, 1024, 8192], P(None, 'row', 'col'), may hold values from -6 to 6
- b_trail: float32 [8192, 8192], P('row', 'col'), may hold values from -6 to 6
- l_cross: float32 [1024, 1024], P('row', 'col'), may hold values from -0.1875 to 0.1875
- l_trail: float32 [2, 8192, 1024], P(None, 'row', 'col'), may hold values from -0.125 to 0.125
- diag_inv: float32 [2, 2, 512, 512], P(None, None, None, 'col'), may hold values from -1.5 to 1.5, as said below
- diag_low: float32 [2, 512, 512], P(None, None, 'col'), may hold values from -0.25 to 0.25
Outputs:
- x_steps: float32 [2, 1024, 8192], P(None, 'row', 'col')
- trail_out: float32 [8192, 8192], P('row', 'col')
Inputs may be any that keep to these rules, and one draw needn't show every extreme that they name: Each diag_inv[s, h] is lower triangular with diagonal entries of 0.5 to 1.5 and strictly lower entries of magnitude at most 3 / sqrt(512).
All inputs are finite; a program needn't handle non-finite values.
Results may differ from a plain program's by a relative error of at most 0.00013.
Values sent between devices are 32-bit elements; how exact they have to be, the bound alone decides.
A program may use at most 64 MiB of HBM per device.

v0:
```python
import jax
import jax.numpy as jnp
from jax import lax
from jax.sharding import PartitionSpec as P

exact_prec = lax.Precision.HIGHEST


def mult(left_mat, right_mat):
    return jnp.dot(left_mat, right_mat, precision=exact_prec, preferred_element_type=jnp.float32)


def inverse_columns(diag_inv, diag_low, section, offset, own_rows):
    inv_first = diag_inv[section, 0]
    inv_second = diag_inv[section, 1]
    low_block = diag_low[section]
    second_all, low_all = (
        lax.all_gather(inv_second, "col", axis=1, tiled=True),
        lax.all_gather(low_block, "col", axis=1, tiled=True),
    )
    left_cols = jnp.concatenate([inv_first, -mult(second_all, mult(low_all, inv_first))], 0)
    right_cols = jnp.concatenate([jnp.zeros_like(inv_second), inv_second], 0)
    left_all, right_all = (
        lax.all_gather(left_cols, "col", axis=1, tiled=True),
        lax.all_gather(right_cols, "col", axis=1, tiled=True),
    )
    whole = jnp.concatenate([left_all, right_all], 1)
    return lax.dynamic_slice_in_dim(whole, offset, own_rows, 1)


def solve_step(diag_inv, diag_low, section, offset, own_rows, rows_block):
    inverse_cols = inverse_columns(diag_inv, diag_low, section, offset, own_rows)
    return lax.psum(mult(inverse_cols, rows_block), "row")


def shards(b_steps, b_trail, l_cross, l_trail, diag_inv, diag_low):
    own_rows = b_steps.shape[1]
    offset = lax.axis_index("row") * own_rows
    solved_first = solve_step(diag_inv, diag_low, 0, offset, own_rows, b_steps[0])
    segment = solved_first
    next_rows = b_steps[1] - mult(lax.all_gather(l_cross, "col", axis=1, tiled=True), segment)
    trail = b_trail - mult(lax.all_gather(l_trail[0], "col", axis=1, tiled=True), segment)
    solved_second = solve_step(diag_inv, diag_low, 1, offset, own_rows, next_rows)
    segment = solved_second
    trail = trail - mult(lax.all_gather(l_trail[1], "col", axis=1, tiled=True), segment)
    mine_first = lax.dynamic_slice_in_dim(solved_first, offset, own_rows, 0)
    mine_second = lax.dynamic_slice_in_dim(solved_second, offset, own_rows, 0)
    return (jnp.stack([mine_first, mine_second]), trail)


def solution(mesh):
    placed = (
        P(None, "row", "col"),
        P("row", "col"),
        P("row", "col"),
        P(None, "row", "col"),
        P(None, None, None, "col"),
        P(None, None, "col"),
    )
    return jax.shard_map(
        shards,
        mesh=mesh,
        in_specs=placed,
        out_specs=(P(None, "row", "col"), P("row", "col")),
        check_vma=False,
    )
```

profile of v0, /device:TPU:1, one launch (start us, length us, event | category | flops | bytes accessed | tf_op | source)
XLA Modules:
  0.0 1003.2 jit_solution(6268098617561068982)
XLA Ops:
  7.2 1.4 fusion.38
  8.7 1.4 slice_bitcast_fusion.4
  10.9 82.2 %all-gather.25.cloned.1.call-done = f32[1,512,512]{1,2,0:T(8,128)} async-done(((f32[1,512,16]{1,2,0:T(8,128)}), f32[1,512,512]{1,2,0:T(8,128)}) %all-gather.25.cloned.1.call-update) | async-done | bytes 1048592 | tf_op jit(solution)/shard_map/all_gather | solution.py:19
  93.1 3.0 fusion.23
  96.2 74.2 %all-gather.27.cloned.1.call-done = f32[1,1,512,512]{2,3,1,0:T(8,128)} async-done(((f32[1,1,512,16]{2,3,1,0:T(8,128)}), f32[1,1,512,512]{2,3,1,0:T(8,128)}) %all-gather.27.cloned.1.call-update) | async-done | bytes 1048592 | tf_op jit(solution)/shard_map/all_gather | solution.py:18
  170.4 1.8 fusion.18
  174.1 76.5 %all-gather.19.cloned.1.call-done = f32[1024,512]{0,1:T(8,128)} async-done(((f32[1024,16]{0,1:T(8,128)}), f32[1024,512]{0,1:T(8,128)}) %all-gather.19.cloned.1.call-update) | async-done | bytes 2097168 | tf_op jit(solution)/shard_map/all_gather | solution.py:25
  250.6 79.8 %all-gather.17.cloned.1.call-done = f32[1024,512]{0,1:T(8,128)} async-done(((f32[1024,16]{0,1:T(8,128)}), f32[1024,512]{0,1:T(8,128)}) %all-gather.17.cloned.1.call-update) | async-done | bytes 2097168 | tf_op jit(solution)/shard_map/all_gather | solution.py:24
  330.4 3.1 fusion.29
  334.3 72.9 %all-gather.29.cloned.1.call-done = f32[1,512,512]{1,2,0:T(8,128)} async-done(((f32[1,512,16]{1,2,0:T(8,128)}), f32[1,512,512]{1,2,0:T(8,128)}) %all-gather.29.cloned.1.call-update) | async-done | bytes 1048592 | tf_op jit(solution)/shard_map/all_gather | solution.py:19
  407.2 3.0 fusion.20
  410.3 74.1 %all-gather.31.cloned.1.call-done = f32[1,1,512,512]{2,3,1,0:T(8,128)} async-done(((f32[1,1,512,16]{2,3,1,0:T(8,128)}), f32[1,1,512,512]{2,3,1,0:T(8,128)}) %all-gather.31.cloned.1.call-update) | async-done | bytes 1048592 | tf_op jit(solution)/shard_map/all_gather | solution.py:18
  484.3 1.8 fusion.17
  487.7 40.3 %all_gather.41 = f32[128,1024]{0,1:T(8,128)S(1)} all-gather(f32[128,32]{0,1:T(8,128)S(1)} %copy-done.4), channel_id=1, replica_groups=mesh['row'=8,'col'=32] {'col'}, dimensions={1}, use_global_device_ids=true | all-gather | bytes 540672 | tf_op jit(solution)/shard_map/all_gather | solution.py:41
  527.9 34.2 %all-reduce.5.cloned.1.call-done = f32[1024,256]{1,0:T(8,128)} async-done(((f32[1024,256]{1,0:T(8,128)}), f32[1024,256]{1,0:T(8,128)}) %all-reduce.5.cloned.1.call-update) | async-done | bytes 1048592 | tf_op jit(solution)/shard_map/psum | solution.py:33
  562.1 2.2 fusion.16
  564.4 85.6 %all-gather.23.cloned.1.call-done = f32[1024,512]{0,1:T(8,128)} async-done(((f32[1024,16]{0,1:T(8,128)}), f32[1024,512]{0,1:T(8,128)}) %all-gather.23.cloned.1.call-update) | async-done | bytes 2097168 | tf_op jit(solution)/shard_map/all_gather | solution.py:25
  649.9 79.4 %all-gather.21.cloned.1.call-done = f32[1024,512]{0,1:T(8,128)} async-done(((f32[1024,16]{0,1:T(8,128)}), f32[1024,512]{0,1:T(8,128)}) %all-gather.21.cloned.1.call-update) | async-done | bytes 2097168 | tf_op jit(solution)/shard_map/all_gather | solution.py:24
  729.3 3.0 fusion.26
  733.3 82.1 %all-gather.35.cloned.1.call-done = f32[1,1024,1024]{1,2,0:T(8,128)} async-done(((f32[1,1024,32]{1,2,0:T(8,128)}), f32[1,1024,1024]{1,2,0:T(8,128)}) %all-gather.35.cloned.1.call-update) | async-done | bytes 4194320 | tf_op jit(solution)/shard_map/all_gather | solution.py:45
  815.4 76.7 %all-reduce.7.cloned.1.call-done = f32[1024,256]{1,0:T(8,128)} async-done(((f32[1024,256]{1,0:T(8,128)}), f32[1024,256]{1,0:T(8,128)}) %all-reduce.7.cloned.1.call-update) | async-done | bytes 1048592 | tf_op jit(solution)/shard_map/psum | solution.py:33
  892.2 7.1 fusion.13
  899.2 88.0 %all-gather.33.cloned.1.call-done = f32[1,1024,1024]{1,2,0:T(8,128)} async-done(((f32[1,1024,32]{1,2,0:T(8,128)}), f32[1,1024,1024]{1,2,0:T(8,128)}) %all-gather.33.cloned.1.call-update) | async-done | bytes 4194320 | tf_op jit(solution)/shard_map/all_gather | solution.py:42
  987.3 6.1 fusion.10
  (44 shorter events, 8.9 us)
Async XLA Ops:
  7.2 86.0 %all-gather.25.cloned.1.call-start = ((), (), s32[]{:S(2)}) async-start(), calls=%async_computation.6 | async-start | bytes 1081344 | tf_op jit(solution)/shard_map/all_gather | solution.py:19
  8.6 161.7 %all-gather.27.cloned.1.call-start = ((), (), s32[]{:S(2)}) async-start(), calls=%async_computation.7 | async-start | bytes 1081344 | tf_op jit(solution)/shard_map/all_gather | solution.py:18
  10.2 240.4 %all-gather.19.cloned.1.call-start = ((), (), s32[]{:S(2)}) async-start(), calls=%async_computation.1 | async-start | bytes 2162688 | tf_op jit(solution)/shard_map/all_gather | solution.py:25
  10.9 319.5 %all-gather.17.cloned.1.call-start = ((), (), s32[]{:S(2)}) async-start(), calls=%async_computation | async-start | bytes 2162688 | tf_op jit(solution)/shard_map/all_gather | solution.py:24
  172.9 234.4 %all-gather.29.cloned.1.call-start = ((), (), s32[]{:S(2)}) async-start(), calls=%async_computation.8 | async-start | bytes 1081344 | tf_op jit(solution)/shard_map/all_gather | solution.py:19
  173.5 310.9 %all-gather.31.cloned.1.call-start = ((), (), s32[]{:S(2)}) async-start(), calls=%async_computation.9 | async-start | bytes 1081344 | tf_op jit(solution)/shard_map/all_gather | solution.py:18
  174.0 388.1 %all-reduce.5.cloned.1.call-start = ((), (), s32[]{:S(2)}) async-start(), calls=%async_computation.2 | async-start | bytes 2097152 | tf_op jit(solution)/shard_map/psum | solution.py:33
  174.1 312.8 %copy-start.3 = (f32[2,1024,32]{1,2,0:T(8,128)S(1)}, f32[2,1024,32]{1,2,0:T(8,128)}, u32[]{:S(2)}) copy-start(f32[2,1024,32]{1,2,0:T(8,128)} %param.9) | copy-start | bytes 786436
  174.1 313.6 %copy-start.4 = (f32[128,32]{0,1:T(8,128)S(1)}, f32[128,32]{0,1:T(8,128)}, u32[]{:S(2)}) copy-start(f32[128,32]{0,1:T(8,128)} %param.8) | copy-start | bytes 49156
  174.1 388.0 %copy-start.2 = (f32[2,128,256]{2,1,0:T(8,128)S(1)}, f32[2,128,256]{2,1,0:T(8,128)}, u32[]{:S(2)}) copy-start(f32[2,128,256]{2,1,0:T(8,128)} %param.6) | copy-start | bytes 786436
  333.5 316.4 %all-gather.23.cloned.1.call-start = ((), (), s32[]{:S(2)}) async-start(), calls=%async_computation.4 | async-start | bytes 2162688 | tf_op jit(solution)/shard_map/all_gather | solution.py:25
  334.2 395.1 %all-gather.21.cloned.1.call-start = ((), (), s32[]{:S(2)}) async-start(), calls=%async_computation.3 | async-start | bytes 2162688 | tf_op jit(solution)/shard_map/all_gather | solution.py:24
  486.8 328.6 %all-gather.35.cloned.1.call-start = ((), (), s32[]{:S(2)}) async-start(), calls=%async_computation.11 | async-start | bytes 4325376 | tf_op jit(solution)/shard_map/all_gather | solution.py:45
  487.6 404.5 %all-reduce.7.cloned.1.call-start = ((), (), s32[]{:S(2)}) async-start(), calls=%async_computation.5 | async-start | bytes 2097152 | tf_op jit(solution)/shard_map/psum | solution.py:33
  527.9 205.0 %copy-start.1 = (f32[1024,256]{1,0:T(8,128)S(1)}, f32[1024,256]{1,0:T(8,128)}, u32[]{:S(2)}) copy-start(f32[1024,256]{1,0:T(8,128)} %param.7) | copy-start | bytes 3145732
  564.4 169.0 %copy-start = (f32[1024,256]{1,0:T(8,128)S(1)}, f32[1024,256]{1,0:T(8,128)}, u32[]{:S(2)}) copy-start(f32[1024,256]{1,0:T(8,128)} %all-reduce.5.cloned.1.call-done) | copy-start | bytes 3145732
  732.4 254.9 %all-gather.33.cloned.1.call-start = ((), (), s32[]{:S(2)}) async-start(), calls=%async_computation.10 | async-start | bytes 4325376 | tf_op jit(solution)/shard_map/all_gather | solution.py:42
Sparse Core Ops, SparseCore 0:
  11.4 81.7 all-gather.24
  95.9 74.3 all-gather.26
  173.7 76.8 all-gather.18
  253.8 76.5 all-gather.16
  333.0 74.1 all-gather.28
  409.9 74.3 all-gather.30
  487.5 74.5 all-reduce.4
  564.9 84.9 all-gather.22
  652.7 76.5 all-gather.20
  732.0 83.4 all-gather.34
  818.6 73.4 all-reduce.6
  895.4 91.8 all-gather.32
where the time goes:
time: 1000 us
  waiting for transfers between devices  907 us (91%)
  blocking collectives  40.3 us (4%)
  matrix products  31.2 us (3%)
  between operations  14.3 us (1%)
    all_gather x2, waiting for transfers between devices, inverse_columns(): lax.all_gather(right_cols, 'col', axis=1, tiled=True)  162 us
    all_gather x2, waiting for transfers between devices, inverse_columns(): lax.all_gather(left_cols, 'col', axis=1, tiled=True)  159 us
    all_gather x2, waiting for transfers between devices, inverse_columns(): lax.all_gather(low_block, 'col', axis=1, tiled=True)  155 us
    all_gather x2, waiting for transfers between devices, inverse_columns(): lax.all_gather(inv_second, 'col', axis=1, tiled=True)  148 us
    psum x2, waiting for transfers between devices, solve_step(): return lax.psum(mult(inverse_cols, rows_block), 'row')  111 us
    all_gather x1, waiting for transfers between devices, shards(): lax.all_gather(l_trail[0], 'col', axis=1, tiled=True)  88 us
    all_gather x1, waiting for transfers between devices, shards(): lax.all_gather(l_trail[1], 'col', axis=1, tiled=True)  82.1 us
    all_gather x1, blocking collectives, shards(): lax.all_gather(l_cross, 'col', axis=1, tiled=True)  40.3 us
  transfers between devices with their start and end apart: 12, of which 12 were waited for; matrix products, arithmetic and copies ran while one was open for 3% of the time, Pallas kernels for 0%

commit v1 on v0

--- a/solution.py
+++ b/solution.py
@@ -39,7 +39,12 @@
     solved_first = solve_step(diag_inv, diag_low, 0, offset, own_rows, b_steps[0])
     segment = solved_first
     next_rows = b_steps[1] - mult(lax.all_gather(l_cross, "col", axis=1, tiled=True), segment)
-    trail = b_trail - mult(lax.all_gather(l_trail[0], "col", axis=1, tiled=True), segment)
+    trail = b_trail - mult(
+        jnp.concatenate(
+            lax.all_to_all(jnp.stack([l_trail[0]] * lax.axis_size("col")), "col", 0, 0), axis=1
+        ),
+        segment,
+    )
     solved_second = solve_step(diag_inv, diag_low, 1, offset, own_rows, next_rows)
     segment = solved_second
     trail = trail - mult(lax.all_gather(l_trail[1], "col", axis=1, tiled=True), segment)

time: 1000 us -> 933 us (0.933)
  waiting for transfers between devices: 907 us -> 742 us
  blocking collectives: 40.3 us -> 126 us
    all_gather x1 -> x0, waiting for transfers between devices: 88 us -> none  [shards(): lax.all_gather(l_trail[0], 'col', axis=1, tiled=True)]
    all_gather x1, blocking collectives: 40.3 us -> 126 us  [shards(): lax.all_gather(l_cross, 'col', axis=1, tiled=True)]
    all_gather x2, waiting for transfers between devices: 162 us -> 123 us  [inverse_columns(): lax.all_gather(right_cols, 'col', axis=1, tiled=True)]
    psum x2, waiting for transfers between devices: 111 us -> 76.7 us  [solve_step(): return lax.psum(mult(inverse_cols, rows_block), 'row')]
  transfers between devices with their start and end apart: 12 -> 12, of which waited for: 12 -> 10; matrix products, arithmetic and copies ran while one was open for 3% -> 3% of each run, Pallas kernels for 0% -> 0%
where the time goes in v1:
time: 933 us; the launch traced here: 929 us
  waiting for transfers between devices  742 us (80%)
  blocking collectives  126 us (14%)
  matrix products  29.7 us (3%)
  between operations  14 us (2%)
  local copies, waits for them, and re-layouts  9.89 us (1%)
    all_gather x2, waiting for transfers between devices, inverse_columns(): lax.all_gather(left_cols, 'col', axis=1, tiled=True)  159 us
    all_gather x2, waiting for transfers between devices, inverse_columns(): lax.all_gather(low_block, 'col', axis=1, tiled=True)  155 us
    all_gather x2, waiting for transfers between devices, inverse_columns(): lax.all_gather(inv_second, 'col', axis=1, tiled=True)  148 us
    all_gather x1, blocking collectives, shards(): lax.all_gather(l_cross, 'col', axis=1, tiled=True)  126 us
    all_gather x2, waiting for transfers between devices, inverse_columns(): lax.all_gather(right_cols, 'col', axis=1, tiled=True)  123 us
    all_gather x1, waiting for transfers between devices, shards(): lax.all_gather(l_trail[1], 'col', axis=1, tiled=True)  77.6 us
    psum x2, waiting for transfers between devices, solve_step(): return lax.psum(mult(inverse_cols, rows_block), 'row')  76.7 us
    dot_general x9, matrix products, mult(): jnp.dot(left_mat, right_mat, precision=exact_prec, preferred_element_type...  29.7 us
  transfers between devices with their start and end apart: 12, of which 10 were waited for; matrix products, arithmetic and copies ran while one was open for 3% of the time, Pallas kernels for 0%

profile of v1, /device:TPU:1, one launch (start us, length us, event | category | flops | bytes accessed | tf_op | source)
XLA Modules:
  0.0 929.1 jit_solution(17316799114032963552)
XLA Ops:
  7.2 1.4 fusion.31
  8.7 1.4 slice_bitcast_fusion.5
  10.9 82.2 %all-gather.23.cloned.1.call-done = f32[1,512,512]{1,2,0:T(8,128)} async-done(((f32[1,512,16]{1,2,0:T(8,128)}), f32[1,512,512]{1,2,0:T(8,128)}) %all-gather.23.cloned.1.call-update) | async-done | bytes 1048592 | tf_op jit(solution)/shard_map/all_gather | solution.py:19
  93.1 3.0 fusion.16
  96.2 74.2 %all-gather.25.cloned.1.call-done = f32[1,1,512,512]{2,3,1,0:T(8,128)} async-done(((f32[1,1,512,16]{2,3,1,0:T(8,128)}), f32[1,1,512,512]{2,3,1,0:T(8,128)}) %all-gather.25.cloned.1.call-update) | async-done | bytes 1048592 | tf_op jit(solution)/shard_map/all_gather | solution.py:18
  170.4 1.8 fusion.11
  174.1 76.5 %all-gather.17.cloned.1.call-done = f32[1024,512]{0,1:T(8,128)} async-done(((f32[1024,16]{0,1:T(8,128)}), f32[1024,512]{0,1:T(8,128)}) %all-gather.17.cloned.1.call-update) | async-done | bytes 2097168 | tf_op jit(solution)/shard_map/all_gather | solution.py:25
  250.6 79.8 %all-gather.15.cloned.1.call-done = f32[1024,512]{0,1:T(8,128)} async-done(((f32[1024,16]{0,1:T(8,128)}), f32[1024,512]{0,1:T(8,128)}) %all-gather.15.cloned.1.call-update) | async-done | bytes 2097168 | tf_op jit(solution)/shard_map/all_gather | solution.py:24
  330.4 3.1 fusion.22
  334.3 72.9 %all-gather.27.cloned.1.call-done = f32[1,512,512]{1,2,0:T(8,128)} async-done(((f32[1,512,16]{1,2,0:T(8,128)}), f32[1,512,512]{1,2,0:T(8,128)}) %all-gather.27.cloned.1.call-update) | async-done | bytes 1048592 | tf_op jit(solution)/shard_map/all_gather | solution.py:19
  407.2 3.0 fusion.13
  410.3 74.1 %all-gather.29.cloned.1.call-done = f32[1,1,512,512]{2,3,1,0:T(8,128)} async-done(((f32[1,1,512,16]{2,3,1,0:T(8,128)}), f32[1,1,512,512]{2,3,1,0:T(8,128)}) %all-gather.29.cloned.1.call-update) | async-done | bytes 1048592 | tf_op jit(solution)/shard_map/all_gather | solution.py:18
  484.3 1.8 fusion.10
  487.6 2.5 stack.15
  490.1 5.6 all-to-all-start
  495.8 125.9 %all_gather.38 = f32[128,1024]{0,1:T(8,128)S(1)} all-gather(f32[128,32]{0,1:T(8,128)S(1)} %copy-done.4), channel_id=1, replica_groups=mesh['row'=8,'col'=32] {'col'}, dimensions={1}, use_global_device_ids=true | all-gather | bytes 540672 | tf_op jit(solution)/shard_map/all_gather | solution.py:41
  621.7 2.3 fusion.9
  624.0 46.9 %all-gather.21.cloned.1.call-done = f32[1024,512]{0,1:T(8,128)} async-done(((f32[1024,16]{0,1:T(8,128)}), f32[1024,512]{0,1:T(8,128)}) %all-gather.21.cloned.1.call-update) | async-done | bytes 2097168 | tf_op jit(solution)/shard_map/all_gather | solution.py:25
  670.9 79.4 %all-gather.19.cloned.1.call-done = f32[1024,512]{0,1:T(8,128)} async-done(((f32[1024,16]{0,1:T(8,128)}), f32[1024,512]{0,1:T(8,128)}) %all-gather.19.cloned.1.call-update) | async-done | bytes 2097168 | tf_op jit(solution)/shard_map/all_gather | solution.py:24
  750.3 3.0 fusion.19
  753.8 5.6 fusion.8
  759.4 77.6 %all-gather.31.cloned.1.call-done = f32[1,1024,1024]{1,2,0:T(8,128)} async-done(((f32[1,1024,32]{1,2,0:T(8,128)}), f32[1,1024,1024]{1,2,0:T(8,128)}) %all-gather.31.cloned.1.call-update) | async-done | bytes 4194320 | tf_op jit(solution)/shard_map/all_gather | solution.py:50
  837.0 76.7 %all-reduce.7.cloned.1.call-done = f32[1024,256]{1,0:T(8,128)} async-done(((f32[1024,256]{1,0:T(8,128)}), f32[1024,256]{1,0:T(8,128)}) %all-reduce.7.cloned.1.call-update) | async-done | bytes 1048592 | tf_op jit(solution)/shard_map/psum | solution.py:33
  913.8 5.9 fusion.5
  (44 shorter events, 8.3 us)
Async XLA Ops:
  7.2 86.0 %all-gather.23.cloned.1.call-start = ((), (), s32[]{:S(2)}) async-start(), calls=%async_computation.7 | async-start | bytes 1081344 | tf_op jit(solution)/shard_map/all_gather | solution.py:19
  8.6 161.7 %all-gather.25.cloned.1.call-start = ((), (), s32[]{:S(2)}) async-start(), calls=%async_computation.8 | async-start | bytes 1081344 | tf_op jit(solution)/shard_map/all_gather | solution.py:18
  10.1 240.4 %all-gather.17.cloned.1.call-start = ((), (), s32[]{:S(2)}) async-start(), calls=%async_computation.2 | async-start | bytes 2162688 | tf_op jit(solution)/shard_map/all_gather | solution.py:25
  10.9 319.5 %all-gather.15.cloned.1.call-start = ((), (), s32[]{:S(2)}) async-start(), calls=%async_computation.1 | async-start | bytes 2162688 | tf_op jit(solution)/shard_map/all_gather | solution.py:24
  172.9 234.4 %all-gather.27.cloned.1.call-start = ((), (), s32[]{:S(2)}) async-start(), calls=%async_computation.9 | async-start | bytes 1081344 | tf_op jit(solution)/shard_map/all_gather | solution.py:19
  173.5 310.9 %all-gather.29.cloned.1.call-start = ((), (), s32[]{:S(2)}) async-start(), calls=%async_computation.10 | async-start | bytes 1081344 | tf_op jit(solution)/shard_map/all_gather | solution.py:18
  174.0 447.6 %all-reduce.5.cloned.1.call-start = ((), (), s32[]{:S(2)}) async-start(), calls=%async_computation.3 | async-start | bytes 2097152 | tf_op jit(solution)/shard_map/psum | solution.py:33
  174.1 312.8 %copy-start.3 = (f32[2,1024,32]{1,2,0:T(8,128)S(1)}, f32[2,1024,32]{1,2,0:T(8,128)}, u32[]{:S(2)}) copy-start(f32[2,1024,32]{1,2,0:T(8,128)} %param.9) | copy-start | bytes 786436
  333.5 337.4 %all-gather.21.cloned.1.call-start = ((), (), s32[]{:S(2)}) async-start(), calls=%async_computation.5 | async-start | bytes 2162688 | tf_op jit(solution)/shard_map/all_gather | solution.py:25
  334.2 416.1 %all-gather.19.cloned.1.call-start = ((), (), s32[]{:S(2)}) async-start(), calls=%async_computation.4 | async-start | bytes 2162688 | tf_op jit(solution)/shard_map/all_gather | solution.py:24
  486.8 350.2 %all-gather.31.cloned.1.call-start = ((), (), s32[]{:S(2)}) async-start(), calls=%async_computation.11 | async-start | bytes 4325376 | tf_op jit(solution)/shard_map/all_gather | solution.py:50
  490.1 5.7 copy-start.4
  490.1 131.6 %copy-start.2 = (f32[2,128,256]{2,1,0:T(8,128)S(1)}, f32[2,128,256]{2,1,0:T(8,128)}, u32[]{:S(2)}) copy-start(f32[2,128,256]{2,1,0:T(8,128)} %param.6) | copy-start | bytes 786436
  490.1 263.7 %all-to-all-start = ((f32[32,1024,32]{1,2,0:T(8,128)}), f32[32,1024,32]{1,2,0:T(8,128)}, u32[]{:S(2)}, u32[]{:S(2)}) async-start(f32[32,1024,32]{1,2,0:T(8,128)} %stack.15), calls=%async_computation | async-start | bytes 8388608 | tf_op jit(solution)/shard_map/all_to_all | solution.py:44
  495.7 418.0 %all-reduce.7.cloned.1.call-start = ((), (), s32[]{:S(2)}) async-start(), calls=%async_computation.6 | async-start | bytes 2097152 | tf_op jit(solution)/shard_map/psum | solution.py:33
  621.7 131.7 %copy-start.1 = (f32[1024,256]{1,0:T(8,128)S(1)}, f32[1024,256]{1,0:T(8,128)}, u32[]{:S(2)}) copy-start(f32[1024,256]{1,0:T(8,128)} %param.7) | copy-start | bytes 3145732
  624.0 129.7 %copy-start = (f32[1024,256]{1,0:T(8,128)S(1)}, f32[1024,256]{1,0:T(8,128)}, u32[]{:S(2)}) copy-start(f32[1024,256]{1,0:T(8,128)} %all-reduce.5.cloned.1.call-done) | copy-start | bytes 3145732
Sparse Core Ops, SparseCore 0:
  11.4 81.7 all-gather.22
  95.9 74.3 all-gather.24
  173.7 76.8 all-gather.16
  253.8 76.5 all-gather.14
  333.0 74.1 all-gather.26
  409.9 74.3 all-gather.28
  487.5 97.3 all-reduce.4
  587.7 83.1 all-gather.20
  673.7 76.5 all-gather.18
  753.5 83.4 all-gather.30
  840.2 73.4 all-reduce.6
